TPU v7x, 32 devices: a whole 2x2x4 slice. The times are simulated.
32 devices in a mesh: grp: 2 (over y), chan: 4 (over z), col: 2 (over x), sub: 2 (over core).
Axes of the slice: x: 2, y: 2, z: 4, core: 2. Of those that a mesh axis runs over, the one named last changes fastest.
Arguments:
- generator: float32 [8, 1024, 1024], P(('grp', 'chan'), 'sub', 'col'), parts along dimension 0, may hold values from -2 to 2
- interaction: float32 [8, 1024, 1024], P(('grp', 'chan'), 'sub', 'col'), parts along dimension 0, may hold values from -2 to 2
- occupations: int32 [160], replicated, may hold values 0 or 1
- pair_orbits: int32 [4, 2, 1024], P('chan'), may hold values from 0 to 159
- cross_orbits: int32 [4, 2, 1024], P('chan'), may hold values from 0 to 159
- pair_sizes: int32 [4], P('chan'), may hold values from 256 to 1024
- cross_sizes: int32 [4], P('chan'), may hold values from 256 to 1024
- cross_target: int32 [4, 32, 8], P('chan', 'sub', 'col'), may hold values from 0 to 255, as said below
Outputs:
- commutator: float32 [8, 1024, 1024], P(('grp', 'chan'), 'sub', 'col'), parts along dimension 0
There are 2 independent parts, one for each index of `grp`. A program takes and returns all parts, laid end to end along the dimension named above; an argument that names none is the same for every part. Nothing has to cross between parts.
Inputs may be any that keep to these rules, and one draw needn't show every extreme that they name: `cross_target`: each value is d * 64 + j: the tile goes to crossed channel d as tile j of the block with the same rows and columns as its own (tiles numbered row by row within the block). Every tile of every crossed channel receives exactly one tile. At most 32 tiles of one block go to one crossed channel, and in every block some crossed channel receives exactly 32.
All inputs are finite; a program needn't handle non-finite values.
Results may differ from a plain program's by a relative error of at most 0.0003.
Values sent between devices are 32-bit elements; how exact they have to be, the bound alone decides.
A program may use at most 64 MiB of HBM per device.

v0:
```python
import jax
import jax.numpy as jnp
from jax import lax
from jax.sharding import PartitionSpec as P

TR = 32
TC = 128


def occupancy(orbit_pairs, occupations, size_limit, particle):
    orbit_ids = jnp.arange(occupations.shape[0], dtype=jnp.int32)
    filled = occupations.astype(jnp.float32)
    matches = (orbit_pairs[:, :, None] == orbit_ids[None, None, :]).astype(jnp.float32)
    looked_up = jnp.sum(matches * filled[None, None, :], axis=2)
    if particle:
        factor = 1.0 - looked_up[0] - looked_up[1]
    else:
        factor = looked_up[0] - looked_up[1]
    position_ids = jnp.arange(orbit_pairs.shape[1], dtype=jnp.int32)
    return factor * (position_ids < size_limit).astype(jnp.float32)


def split_tiles(matrix):
    height = matrix.shape[0] // TR
    breadth = matrix.shape[1] // TC
    return (
        matrix.reshape(height, TR, breadth, TC)
        .transpose(0, 2, 1, 3)
        .reshape(height * breadth, TR, TC)
    )


def join_tiles(tiles, height, breadth):
    return (
        tiles.reshape(height, breadth, TR, TC)
        .transpose(0, 2, 1, 3)
        .reshape(height * TR, breadth * TC)
    )


def make_accumulate(column_generator, column_interaction, weights, pieces):
    piece_generator, piece_interaction = pieces
    forward = jnp.dot(
        piece_generator * weights[None, :],
        column_interaction,
        precision=lax.Precision.HIGHEST,
        preferred_element_type=jnp.float32,
    )
    reverse = jnp.dot(
        piece_interaction * weights[None, :],
        column_generator,
        precision=lax.Precision.HIGHEST,
        preferred_element_type=jnp.float32,
    )
    return forward - reverse


def shards(
    generator,
    interaction,
    occupations,
    pair_orbits,
    cross_orbits,
    pair_sizes,
    cross_sizes,
    cross_target,
):
    row_count = generator.shape[1]
    column_width = generator.shape[2]
    channel_count = lax.axis_size("chan")
    row_tiles = row_count // TR
    col_tiles = column_width // TC
    tile_count = row_tiles * col_tiles
    capacity = 2 * tile_count // channel_count
    row_index = lax.axis_index("sub") * row_count + jnp.arange(row_count, dtype=jnp.int32)
    col_index = lax.axis_index("col") * column_width + jnp.arange(column_width, dtype=jnp.int32)
    live_block = (
        (row_index < pair_sizes[0])[:, None] & (col_index < pair_sizes[0])[None, :]
    ).astype(jnp.float32)
    generator_live = generator[0] * live_block
    interaction_live = interaction[0] * live_block
    pair_weight = occupancy(pair_orbits[0], occupations, pair_sizes[0], True)
    cross_weight = occupancy(cross_orbits[0], occupations, cross_sizes[0], False)
    column_generator, column_interaction = (
        lax.all_gather(generator_live, "sub", axis=0, tiled=True),
        lax.all_gather(interaction_live, "sub", axis=0, tiled=True),
    )
    particle = make_accumulate(
        column_generator,
        column_interaction,
        pair_weight,
        (
            lax.all_gather(generator_live, "col", axis=1, tiled=True),
            lax.all_gather(interaction_live, "col", axis=1, tiled=True),
        ),
    )
    targets = cross_target[0].reshape(-1)
    owner_of = targets // tile_count
    slot_of = targets % tile_count
    owner_hits = (owner_of[:, None] == jnp.arange(channel_count, dtype=jnp.int32)[None, :]).astype(
        jnp.int32
    )
    earlier = jnp.sum((jnp.cumsum(owner_hits, axis=0) - owner_hits) * owner_hits, axis=1)
    position = owner_of * capacity + earlier

    def pack(block):
        buffer = (
            jnp.zeros((channel_count * capacity, TR, TC), jnp.float32)
            .at[position]
            .set(split_tiles(block))
        )
        return buffer.reshape(channel_count, capacity, TR, TC)

    slot_buffer = (
        jnp.full((channel_count * capacity,), -1.0, jnp.float32)
        .at[position]
        .set(slot_of.astype(jnp.float32))
        .reshape(channel_count, capacity)
    )
    got_generator, got_interaction, owner_slots = (
        lax.all_to_all(pack(generator_live), "chan", split_axis=0, concat_axis=0, tiled=True),
        lax.all_to_all(pack(interaction_live), "chan", split_axis=0, concat_axis=0, tiled=True),
        lax.all_to_all(slot_buffer, "chan", split_axis=0, concat_axis=0, tiled=True),
    )
    flat_slots = owner_slots.reshape(-1)
    placed = jnp.where(flat_slots >= 0, flat_slots, tile_count).astype(jnp.int32)
    empty_tiles = jnp.zeros((tile_count, TR, TC), jnp.float32)
    crossed_generator = join_tiles(
        empty_tiles.at[placed].set(got_generator.reshape(-1, TR, TC), mode="drop"),
        row_tiles,
        col_tiles,
    )
    crossed_interaction = join_tiles(
        empty_tiles.at[placed].set(got_interaction.reshape(-1, TR, TC), mode="drop"),
        row_tiles,
        col_tiles,
    )
    cross_column_generator, cross_column_interaction = (
        lax.all_gather(crossed_generator, "sub", axis=0, tiled=True),
        lax.all_gather(crossed_interaction, "sub", axis=0, tiled=True),
    )
    crossed = make_accumulate(
        cross_column_generator,
        cross_column_interaction,
        cross_weight,
        (
            lax.all_gather(crossed_generator, "col", axis=1, tiled=True),
            lax.all_gather(crossed_interaction, "col", axis=1, tiled=True),
        ),
    )
    flat_owner_slots = owner_slots.reshape(-1)
    valid_slots = (flat_owner_slots >= 0).astype(jnp.float32)
    picked = jnp.where(flat_owner_slots >= 0, flat_owner_slots, 0.0).astype(jnp.int32)
    back_buffer = (split_tiles(crossed)[picked] * valid_slots[:, None, None]).reshape(
        channel_count, capacity, TR, TC
    )
    returned_tiles = lax.all_to_all(back_buffer, "chan", split_axis=0, concat_axis=0, tiled=True)
    returned = join_tiles(returned_tiles.reshape(-1, TR, TC)[position], row_tiles, col_tiles)
    return (live_block * (particle - returned))[None]


def solution(mesh):
    return jax.shard_map(
        shards,
        mesh=mesh,
        in_specs=(
            P(("grp", "chan"), "sub", "col"),
            P(("grp", "chan"), "sub", "col"),
            P(),
            P("chan", None, None),
            P("chan", None, None),
            P("chan"),
            P("chan"),
            P("chan", "sub", "col"),
        ),
        out_specs=P(("grp", "chan"), "sub", "col"),
        check_vma=False,
    )
```

profile of v0, /device:TPU:17, one launch (start us, length us, event | category | flops | bytes accessed | tf_op | source)
XLA Modules:
  0.0 308.0 jit_solution(5519818243890734875)
XLA Ops:
  9.4 4.6 %all-to-all-start = ((f32[4,1,32]{2,1,0:T(1,128)}), f32[4,1,32]{2,1,0:T(1,128)S(1)}, u32[]{:S(2)}, u32[]{:S(2)}) async-start(f32[4,1,32]{2,1,0:T(1,128)} %bitcast.7), calls=%async_computation | async-start | bytes 4096 | tf_op jit(solution)/shard_map/all_to_all | solution.py:123
  19.9 8.1 %scatter_fusion.2 = f32[128,32,128]{2,1,0:T(8,128)} fusion(f32[128,32,128]{2,1,0:T(8,128)} %broadcast.262.clone.1, s32[64]{0:T(128)S(1)} %fusion.30, f32[64,32,128]{2,1,0:T(8,128)S(1)} %bitcast.84), kind=kCustom, calls=%fused_computation.5 | custom fusion | bytes 3145984 | tf_op jit(solution)/shard_map/scatter | solution.py:110
  28.1 4.5 %all-to-all-start.2 = ((f32[4,32,32,128]{3,2,1,0:T(8,128)}), f32[4,32,32,128]{3,2,1,0:T(8,128)S(1)}, u32[]{:S(2)}, u32[]{:S(2)}) async-start(f32[4,32,32,128]{3,2,1,0:T(8,128)} %bitcast.20), calls=%async_computation.2 | async-start | bytes 4194304 | tf_op jit(solution)/shard_map/all_to_all | solution.py:122
  34.0 1.6 broadcast.262.clone
  35.6 8.1 %scatter_fusion = f32[128,32,128]{2,1,0:T(8,128)} fusion(f32[128,32,128]{2,1,0:T(8,128)} %broadcast.262.clone, s32[64]{0:T(128)S(1)} %fusion.30, f32[64,32,128]{2,1,0:T(8,128)S(1)} %bitcast.85), kind=kCustom, calls=%fused_computation.3 | custom fusion | bytes 3145984 | tf_op jit(solution)/shard_map/scatter | solution.py:110
  43.7 33.7 %all-to-all-done.2 = f32[4,32,32,128]{3,2,1,0:T(8,128)S(1)} async-done(((f32[4,32,32,128]{3,2,1,0:T(8,128)}), f32[4,32,32,128]{3,2,1,0:T(8,128)S(1)}, u32[]{:S(2)}, u32[]{:S(2)}) %all-to-all-start.2) | async-done | bytes 2097184 | tf_op jit(solution)/shard_map/all_to_all | solution.py:122
  78.7 6.6 %all-to-all-start.1 = ((f32[4,32,32,128]{3,2,1,0:T(8,128)}), f32[4,32,32,128]{3,2,1,0:T(8,128)S(1)}, u32[]{:S(2)}, u32[]{:S(2)}) async-start(f32[4,32,32,128]{3,2,1,0:T(8,128)} %bitcast.11), calls=%async_computation.1 | async-start | bytes 4194304 | tf_op jit(solution)/shard_map/all_to_all | solution.py:121
  86.6 12.0 %scatter_fusion.3 = f32[64,32,128]{2,1,0:T(8,128)S(1)} fusion(f32[64,32,128]{2,1,0:T(8,128)S(1)} %broadcast_in_dim.10.clone.1, s32[128]{0:T(128)S(1)} %get-tuple-element.12, f32[128,32,128]{2,1,0:T(8,128)} %bitcast.79), kind=kCustom, calls=%fused_computation.6 | custom fusion | bytes 6291968 | tf_op jit(solution)/shard_map/scatter | solution.py:134
  100.4 29.6 %all-to-all-done.1 = f32[4,32,32,128]{3,2,1,0:T(8,128)S(1)} async-done(((f32[4,32,32,128]{3,2,1,0:T(8,128)}), f32[4,32,32,128]{3,2,1,0:T(8,128)S(1)}, u32[]{:S(2)}, u32[]{:S(2)}) %all-to-all-start.1) | async-done | bytes 2097184 | tf_op jit(solution)/shard_map/all_to_all | solution.py:121
  130.1 4.6 %scatter_fusion.1 = f32[64,32,128]{2,1,0:T(8,128)S(1)} fusion(f32[64,32,128]{2,1,0:T(8,128)S(1)} %broadcast_in_dim.10.clone, s32[128]{0:T(128)S(1)} %get-tuple-element.12, f32[128,32,128]{2,1,0:T(8,128)S(1)} %bitcast.78), kind=kCustom, calls=%fused_computation.4 | custom fusion | bytes 6291968 | tf_op jit(solution)/shard_map/scatter | solution.py:129
  142.2 8.4 %all-gather.23.cloned.1.call-done = f32[1024,512]{1,0:T(8,128)} async-done(((f32[512,512]{1,0:T(8,128)}), f32[1024,512]{1,0:T(8,128)}) %all-gather.23.cloned.1.call-update) | async-done | bytes 2097168 | tf_op jit(solution)/shard_map/all_gather | solution.py:139
  150.6 5.8 %fusion = f32[512,512]{1,0:T(8,128)S(1)} fusion(f32[1024,512]{1,0:T(8,128)} %all-gather.23.cloned.1.call-done, f32[512,1024]{1,0:T(8,128)} %all-gather.21.cloned.1.call-done, f32[1024]{0:T(1024)S(1)} %bitcast.90), kind=kOutput, calls=%fused_computation.7 | convolution fusion | flops 3221749760 | bytes 5246976 | tf_op jit(solution)/shard_map/dot_general | solution.py:49
  156.3 29.2 %all-gather.17.cloned.1.call-done = f32[512,1024]{1,0:T(8,128)} async-done(((f32[512,512]{1,0:T(8,128)}), f32[512,1024]{1,0:T(8,128)}) %all-gather.17.cloned.1.call-update) | async-done | bytes 2097168 | tf_op jit(solution)/shard_map/all_gather | solution.py:147
  185.5 12.9 %all-gather.19.cloned.1.call-done = f32[1024,512]{1,0:T(8,128)} async-done(((f32[512,512]{1,0:T(8,128)}), f32[1024,512]{1,0:T(8,128)}) %all-gather.19.cloned.1.call-update) | async-done | bytes 2097168 | tf_op jit(solution)/shard_map/all_gather | solution.py:140
  198.4 5.8 %fusion.11 = f32[512,512]{1,0:T(8,128)S(1)} fusion(f32[512,512]{1,0:T(8,128)S(1)} %fusion, f32[1024,512]{1,0:T(8,128)} %all-gather.19.cloned.1.call-done, f32[512,1024]{1,0:T(8,128)} %all-gather.17.cloned.1.call-done, f32[1024]{0:T(1024)S(1)} %bitcast.91), kind=kOutput, calls=%fused_computation.19 | convolution fusion | flops 3222011904 | bytes 6295552 | tf_op jit(solution)/shard_map/dot_general | solution.py:43
  205.5 1.6 broadcast_multiply_fusion
  207.1 4.6 %all-to-all-start.3 = ((f32[4,32,32,128]{3,2,1,0:T(8,128)}), f32[4,32,32,128]{3,2,1,0:T(8,128)S(1)}, u32[]{:S(2)}, u32[]{:S(2)}) async-start(f32[4,32,32,128]{3,2,1,0:T(8,128)} %broadcast_multiply_fusion), calls=%async_computation.3 | async-start | bytes 4194304 | tf_op jit(solution)/shard_map/all_to_all | solution.py:157
  212.4 20.8 %all-gather.13.cloned.1.call-done = f32[512,1024]{1,0:T(8,128)} async-done(((f32[512,512]{1,0:T(8,128)}), f32[512,1024]{1,0:T(8,128)}) %all-gather.13.cloned.1.call-update) | async-done | bytes 2097168 | tf_op jit(solution)/shard_map/all_gather | solution.py:94
  233.2 12.9 %all-gather.15.cloned.1.call-done = f32[1024,512]{1,0:T(8,128)} async-done(((f32[512,512]{1,0:T(8,128)}), f32[1024,512]{1,0:T(8,128)}) %all-gather.15.cloned.1.call-update) | async-done | bytes 2097168 | tf_op jit(solution)/shard_map/all_gather | solution.py:85
  246.1 6.7 %fusion.4 = f32[512,512]{1,0:T(8,128)} fusion(f32[1024,512]{1,0:T(8,128)} %all-gather.15.cloned.1.call-done, f32[512,1024]{1,0:T(8,128)} %all-gather.13.cloned.1.call-done, f32[1024]{0:T(1024)S(1)} %bitcast.88), kind=kOutput, calls=%fused_computation.11 | convolution fusion | flops 3221749760 | bytes 5246976 | tf_op jit(solution)/shard_map/dot_general | solution.py:49
  252.8 3.6 %all-to-all-done.3 = f32[4,32,32,128]{3,2,1,0:T(8,128)S(1)} async-done(((f32[4,32,32,128]{3,2,1,0:T(8,128)}), f32[4,32,32,128]{3,2,1,0:T(8,128)S(1)}, u32[]{:S(2)}, u32[]{:S(2)}) %all-to-all-start.3) | async-done | bytes 2097184 | tf_op jit(solution)/shard_map/all_to_all | solution.py:157
  257.8 1.6 all-gather.11.cloned.1.call-done
  259.4 35.0 %all-gather.9.cloned.1.call-done = f32[512,1024]{1,0:T(8,128)} async-done(((f32[512,512]{1,0:T(8,128)}), f32[512,1024]{1,0:T(8,128)}) %all-gather.9.cloned.1.call-update) | async-done | bytes 2097168 | tf_op jit(solution)/shard_map/all_gather | solution.py:93
  294.4 6.8 %fusion.19 = f32[1,512,512]{2,1,0:T(8,128)} fusion(f32[512,512]{1,0:T(8,128)S(1)} %copy-done.4, f32[1024,512]{1,0:T(8,128)} %all-gather.11.cloned.1.call-done, f32[512,1024]{1,0:T(8,128)} %all-gather.9.cloned.1.call-done, f32[64,8,4,128]{3,2,1,0:T(4,128)S(1)} %bitcast.82, f32[1024]{0:T(1024)S(1)} %bitcast.89, pred[512]{0:T(512)(128)(4,1)S(1)} %get-tuple-element.15, ...), kind=kOutput, calls=%fused_computation.21 | convolution fusion | flops 3222798336 | bytes 7345152 | tf_op jit(solution)/shard_map/dot_general | solution.py:43
  (76 shorter events, 24.0 us)
Async XLA Ops:
  6.5 9.7 %copy-start.1 = (f32[1,512,512]{2,1,0:T(8,128)S(1)}, f32[1,512,512]{2,1,0:T(8,128)}, u32[]{:S(2)}) copy-start(f32[1,512,512]{2,1,0:T(8,128)} %param.9) | copy-start | bytes 3145732
  9.4 18.7 %all-to-all-start = ((f32[4,1,32]{2,1,0:T(1,128)}), f32[4,1,32]{2,1,0:T(1,128)S(1)}, u32[]{:S(2)}, u32[]{:S(2)}) async-start(f32[4,1,32]{2,1,0:T(1,128)} %bitcast.7), calls=%async_computation | async-start | bytes 4096 | tf_op jit(solution)/shard_map/all_to_all | solution.py:123
  28.1 49.3 %all-to-all-start.2 = ((f32[4,32,32,128]{3,2,1,0:T(8,128)}), f32[4,32,32,128]{3,2,1,0:T(8,128)S(1)}, u32[]{:S(2)}, u32[]{:S(2)}) async-start(f32[4,32,32,128]{3,2,1,0:T(8,128)} %bitcast.20), calls=%async_computation.2 | async-start | bytes 4194304 | tf_op jit(solution)/shard_map/all_to_all | solution.py:122
  77.4 1.3 copy-start
  78.7 51.3 %all-to-all-start.1 = ((f32[4,32,32,128]{3,2,1,0:T(8,128)}), f32[4,32,32,128]{3,2,1,0:T(8,128)S(1)}, u32[]{:S(2)}, u32[]{:S(2)}) async-start(f32[4,32,32,128]{3,2,1,0:T(8,128)} %bitcast.11), calls=%async_computation.1 | async-start | bytes 4194304 | tf_op jit(solution)/shard_map/all_to_all | solution.py:121
  85.2 56.9 %all-gather.21.cloned.1.call-start = ((), (), s32[]{:S(2)}) async-start(), calls=%async_computation.10 | async-start | bytes 3145728 | tf_op jit(solution)/shard_map/all_gather | solution.py:148
  100.4 50.2 %all-gather.23.cloned.1.call-start = ((), (), s32[]{:S(2)}) async-start(), calls=%async_computation.11 | async-start | bytes 3145728 | tf_op jit(solution)/shard_map/all_gather | solution.py:139
  136.5 1.4 copy-start.2
  136.5 1.5 copy-start.3
  136.5 49.0 %all-gather.17.cloned.1.call-start = ((), (), s32[]{:S(2)}) async-start(), calls=%async_computation.8 | async-start | bytes 3145728 | tf_op jit(solution)/shard_map/all_gather | solution.py:147
  137.3 61.1 %all-gather.19.cloned.1.call-start = ((), (), s32[]{:S(2)}) async-start(), calls=%async_computation.9 | async-start | bytes 3145728 | tf_op jit(solution)/shard_map/all_gather | solution.py:140
  137.8 95.4 %all-gather.13.cloned.1.call-start = ((), (), s32[]{:S(2)}) async-start(), calls=%async_computation.6 | async-start | bytes 3145728 | tf_op jit(solution)/shard_map/all_gather | solution.py:94
  139.6 1.4 copy-start.7
  139.6 2.0 copy-start.5
  139.6 2.0 copy-start.6
  139.6 106.5 %all-gather.15.cloned.1.call-start = ((), (), s32[]{:S(2)}) async-start(), calls=%async_computation.7 | async-start | bytes 3145728 | tf_op jit(solution)/shard_map/all_gather | solution.py:85
  140.2 119.2 %all-gather.11.cloned.1.call-start = ((), (), s32[]{:S(2)}) async-start(), calls=%async_computation.5 | async-start | bytes 3145728 | tf_op jit(solution)/shard_map/all_gather | solution.py:86
  207.1 49.4 %all-to-all-start.3 = ((f32[4,32,32,128]{3,2,1,0:T(8,128)}), f32[4,32,32,128]{3,2,1,0:T(8,128)S(1)}, u32[]{:S(2)}, u32[]{:S(2)}) async-start(f32[4,32,32,128]{3,2,1,0:T(8,128)} %broadcast_multiply_fusion), calls=%async_computation.3 | async-start | bytes 4194304 | tf_op jit(solution)/shard_map/all_to_all | solution.py:157
  211.6 82.7 %all-gather.9.cloned.1.call-start = ((), (), s32[]{:S(2)}) async-start(), calls=%async_computation.4 | async-start | bytes 3145728 | tf_op jit(solution)/shard_map/all_gather | solution.py:93
  257.1 37.3 %copy-start.4 = (f32[512,512]{1,0:T(8,128)S(1)}, f32[512,512]{1,0:T(8,128)}, u32[]{:S(2)}) copy-start(f32[512,512]{1,0:T(8,128)} %fusion.4) | copy-start | bytes 3145732
Sparse Core Ops, SparseCore 0:
  100.5 34.8 all-gather.20
  136.9 13.5 all-gather.22
  152.1 33.3 all-gather.16
  186.9 11.4 all-gather.18
  199.8 33.3 all-gather.12
  234.6 11.4 all-gather.14
  247.6 11.7 all-gather.10
  261.0 33.3 all-gather.8
where the time goes:
time: 311 us; the launch traced here: 308 us
  waiting for transfers between devices  191 us (61%)
  local copies, waits for them, and re-layouts  50.2 us (16%)
  matrix products  25.1 us (8%)
  starting transfers between devices  20.7 us (7%)
  between operations  15.1 us (5%)
  other arithmetic  6.32 us (2%)
    all_gather x1, waiting for transfers between devices, shards(): lax.all_gather(generator_live, 'col', axis=1, tiled=True)  35 us
    all_to_all x1, waiting for transfers between devices, shards(): lax.all_to_all(pack(interaction_live), 'chan', split_axis=0, concat_axis=...  33.7 us
    all_to_all x1, waiting for transfers between devices, shards(): lax.all_to_all(pack(generator_live), 'chan', split_axis=0, concat_axis=0,...  29.6 us
    all_gather x1, waiting for transfers between devices, shards(): lax.all_gather(crossed_generator, 'col', axis=1, tiled=True)  29.2 us
    all_gather x1, waiting for transfers between devices, shards(): lax.all_gather(interaction_live, 'col', axis=1, tiled=True)  20.8 us
    scatter x2, local copies, waits for them, and re-layouts, pack(): buffer = jnp.zeros((channel_count * capacity, TR, TC), jnp.float32).at[po...  16.2 us
    all_gather x1, waiting for transfers between devices, shards(): lax.all_gather(crossed_interaction, 'sub', axis=0, tiled=True)  12.9 us
    all_gather x1, waiting for transfers between devices, shards(): lax.all_gather(generator_live, 'sub', axis=0, tiled=True)  12.9 us
  transfers between devices with their start and end apart: 12, of which 10 were waited for; matrix products, arithmetic and copies ran while one was open for 23% of the time, Pallas kernels for 0%

commit v1 on v0

v1 whole, which is shorter than its diff:
```python
import functools

import jax
import jax.numpy as jnp
from jax import lax
from jax.experimental import pallas as pl
from jax.experimental.pallas import tpu as pltpu
from jax.sharding import PartitionSpec as P

TR = 32
TC = 128
LANES = 128
MESH = pl.DeviceIdType.MESH
VMEM_LIMIT = 60 * 1024 * 1024


def split(value):
    high = value.astype(jnp.bfloat16)
    low = (value - high.astype(jnp.float32)).astype(jnp.bfloat16)
    return high, low


def rank_order(count):
    far = sorted(range(1, count), key=lambda d: (-min(d, count - d), -d))
    return far


def kernel(
    sizes,
    gen_ref,
    int_ref,
    pair_orb_ref,
    cross_orb_ref,
    filled_ref,
    size_ref,
    pack_ref,
    ret_ref,
    meta_ref,
    out_ref,
    tiled_g,
    tiled_i,
    send_g,
    send_i,
    raw_g,
    raw_i,
    rawx_g,
    rawx_i,
    raws_g,
    raws_i,
    meta_own,
    meta_x,
    meta_s,
    smeta_own,
    smeta_x,
    smeta_s,
    left_g_hi,
    left_g_lo,
    left_i_hi,
    left_i_lo,
    right_g_hi,
    right_g_lo,
    right_i_hi,
    right_i_lo,
    product,
    back_send,
    back_recv,
    partx,
    parts,
    particle,
    weights,
    z_send,
    z_recv,
    x_send,
    x_recv,
    s_send,
    s_recv,
    m_send,
    m_recv,
    local_sem,
    b_send,
    b_recv,
    p_send,
    p_recv,
):
    n_chan, n_col, n_sub, height, width, cap, chunk = sizes
    n_chunk = cap // chunk
    rt, ct = height // TR, width // TC
    tiles = rt * ct
    me = lax.axis_index("chan")
    my_col = lax.axis_index("col")
    my_sub = lax.axis_index("sub")

    def at(axis, index, count, step):
        return {axis: lax.rem(index + step, count)}

    def to_chan(step):
        return at("chan", me, n_chan, step)

    def to_col(step):
        return at("col", my_col, n_col, step)

    def to_sub(step):
        return at("sub", my_sub, n_sub, step)

    distances = rank_order(n_chan)

    barrier = pltpu.get_barrier_semaphore()
    for d in range(1, n_chan):
        pl.semaphore_signal(barrier, inc=1, device_id=to_chan(d), device_id_type=MESH)
    for d in range(1, n_col):
        pl.semaphore_signal(barrier, inc=1, device_id=to_col(d), device_id_type=MESH)
    for d in range(1, n_sub):
        pl.semaphore_signal(barrier, inc=1, device_id=to_sub(d), device_id_type=MESH)

    limit = size_ref[0]
    row_in = lax.broadcasted_iota(jnp.int32, (TR, TC), 0) + my_sub * height
    col_in = lax.broadcasted_iota(jnp.int32, (TR, TC), 1) + my_col * width

    def live_of(r, t):
        keep = (row_in + r * TR < limit) & (col_in + t * TC < limit)
        return keep.astype(jnp.float32)

    own_meta = pltpu.make_async_copy(meta_ref.at[me], meta_own.at[me], local_sem.at[0])
    own_meta.start()

    def to_tiles(r, carry):
        rows = pl.ds(pl.multiple_of(r * TR, TR), TR)
        for t in range(ct):
            keep = live_of(r, t)
            cols = pl.ds(t * TC, TC)
            tiled_g[r * ct + t] = gen_ref[rows, cols] * keep
            tiled_i[r * ct + t] = int_ref[rows, cols] * keep
        return carry

    lax.fori_loop(0, rt, to_tiles, 0)

    def pack_one(tiled, sent, raw):
        for d in distances:
            base = lax.rem(me + d, n_chan) * cap

            def put(k, carry, base=base, d=d):
                sent[(d - 1) * cap + k] = tiled[pack_ref[base + k]]
                return carry

            lax.fori_loop(0, cap, put, 0, unroll=min(cap, 4))

        def keep_own(k, carry):
            raw[me * cap + k] = tiled[pack_ref[me * cap + k]]
            return carry

        lax.fori_loop(0, cap, keep_own, 0, unroll=min(cap, 4))

    pack_one(tiled_g, send_g, raw_g)
    pack_one(tiled_i, send_i, raw_i)
    pl.semaphore_wait(barrier, n_chan + n_col + n_sub - 3)

    started = []

    def remote(src, dst, ssem, rsem, device):
        copy = pltpu.make_async_remote_copy(
            src_ref=src,
            dst_ref=dst,
            send_sem=ssem,
            recv_sem=rsem,
            device_id=device,
            device_id_type=MESH,
        )
        copy.start()
        started.append(copy)
        return copy

    meta_copies = [
        remote(
            meta_ref.at[lax.rem(me + d, n_chan)],
            meta_own.at[me],
            m_send.at[d - 1],
            m_recv.at[d - 1],
            to_chan(d),
        )
        for d in distances
    ]
    sent = (send_g, send_i)
    raw = (raw_g, raw_i)
    rawx = (rawx_g, rawx_i)
    raws = (raws_g, raws_i)
    z_copies = {}
    for m in range(2):
        for q in range(n_chunk):
            for d in distances:
                z_copies[m, q, d] = remote(
                    sent[m].at[pl.ds((d - 1) * cap + q * chunk, chunk)],
                    raw[m].at[pl.ds(me * cap + q * chunk, chunk)],
                    z_send.at[m, q, d - 1],
                    z_recv.at[m, q, d - 1],
                    to_chan(d),
                )

    x_copies, s_copies = {}, {}

    def forward(m, q, d):
        source = lax.rem(me + n_chan - d, n_chan)
        rows = pl.ds(source * cap + q * chunk, chunk)
        for e in range(1, n_col):
            x_copies[m, q, d, e] = remote(
                raw[m].at[rows],
                rawx[m].at[e - 1, rows],
                x_send.at[m, q, d, e - 1],
                x_recv.at[m, q, d, e - 1],
                to_col(e),
            )
        for e in range(1, n_sub):
            s_copies[m, q, d, e] = remote(
                raw[m].at[rows],
                raws[m].at[e - 1, rows],
                s_send.at[m, q, d, e - 1],
                s_recv.at[m, q, d, e - 1],
                to_sub(e),
            )

    for m in range(2):
        for q in range(n_chunk):
            forward(m, q, 0)

    states = pair_orb_ref.shape[1]

    def look_up(orbit, found):
        value = filled_ref[orbit]
        pair_found, cross_found = found
        pair_found = pair_found + jnp.where(pair_orb_ref[...] == orbit, value, 0.0)
        cross_found = cross_found + jnp.where(cross_orb_ref[...] == orbit, value, 0.0)
        return pair_found, cross_found

    zero = jnp.zeros((2, states), jnp.float32)
    pair_found, cross_found = lax.fori_loop(0, filled_ref.shape[0], look_up, (zero, zero))
    state_id = lax.broadcasted_iota(jnp.int32, (1, states), 1)
    pair_weight = (1.0 - pair_found[0:1] - pair_found[1:2]) * (state_id < limit).astype(jnp.float32)
    cross_weight = (cross_found[0:1] - cross_found[1:2]) * (state_id < size_ref[1]).astype(
        jnp.float32
    )
    for g in range(states // TC):
        weights[0, g] = jnp.broadcast_to(pair_weight[:, g * TC : (g + 1) * TC], (8, TC))
        weights[1, g] = jnp.broadcast_to(cross_weight[:, g * TC : (g + 1) * TC], (8, TC))

    own_meta.wait()
    for copy in meta_copies:
        copy.wait_recv()
    meta_next = []
    for e in range(1, n_col):
        meta_next.append(
            remote(
                meta_own,
                meta_x.at[e - 1],
                m_send.at[n_chan - 1 + e - 1],
                m_recv.at[n_chan - 1 + e - 1],
                to_col(e),
            )
        )
    for e in range(1, n_sub):
        meta_next.append(
            remote(
                meta_own,
                meta_s.at[e - 1],
                m_send.at[n_chan + n_col - 2 + e - 1],
                m_recv.at[n_chan + n_col - 2 + e - 1],
                to_sub(e),
            )
        )
    for copy in meta_next:
        copy.wait_recv()
    scalar_copies = [
        pltpu.make_async_copy(meta_own, smeta_own, local_sem.at[0]),
        pltpu.make_async_copy(meta_x, smeta_x, local_sem.at[1]),
        pltpu.make_async_copy(meta_s, smeta_s, local_sem.at[2]),
    ]
    for copy in scalar_copies:
        copy.start()
    for copy in scalar_copies:
        copy.wait()

    left = ((left_g_hi, left_g_lo), (left_i_hi, left_i_lo))
    right = ((right_g_hi, right_g_lo), (right_i_hi, right_i_lo))

    def put_left(which, m, block, rows, t, value):
        weight = weights[which, block * ct + t][0:1]
        signed = value * (weight if m == 0 else -weight)
        high, low = split(signed)
        cols = pl.ds(t * TC, TC)
        left[m][0][block, rows, cols] = high
        left[m][1][block, rows, cols] = low

    def put_right(m, block, r, t, value):
        rows = pl.ds(pl.multiple_of(block * height + r * TR, TR), TR)
        high, low = split(value)
        cols = pl.ds(t * TC, TC)
        right[m][0][rows, cols] = high
        right[m][1][rows, cols] = low

    def assemble(m, read_tile, slot_of, in_left, in_right):
        def one_row(r, carry):
            rows = pl.ds(pl.multiple_of(r * TR, TR), TR)
            for t in range(ct):
                j = r * ct + t
                where = slot_of(0, j)
                for source in range(1, n_chan):
                    where = where + slot_of(source, j)
                value = read_tile(where)
                if in_left is not None:
                    put_left(1, m, in_left, rows, t, value)
                if in_right is not None:
                    put_right(m, in_right, r, t, value)
            return carry

        lax.fori_loop(0, rt, one_row, 0)

    def assemble_own(m):
        assemble(
            m, lambda w: raw[m][w], lambda source, j: smeta_own[source, 0, j], my_col, my_sub
        )

    def assemble_sub(m):
        for e in range(1, n_sub):
            assemble(
                m,
                lambda w, e=e: raws[m][e - 1, w],
                lambda source, j, e=e: smeta_s[e - 1, source, 0, j],
                None,
                lax.rem(my_sub + n_sub - e, n_sub),
            )

    def assemble_col(m):
        for e in range(1, n_col):
            assemble(
                m,
                lambda w, e=e: rawx[m][e - 1, w],
                lambda source, j, e=e: smeta_x[e - 1, source, 0, j],
                lax.rem(my_col + n_col - e, n_col),
                None,
            )

    def wait_all(copies, m):
        for key, copy in copies.items():
            if key[0] == m:
                copy.wait_recv()

    def take(m, q):
        for d in distances:
            z_copies[m, q, d].wait_recv()
            forward(m, q, d)

    for q in range(n_chunk):
        take(0, q)
    take(1, 0)
    assemble_own(0)
    if n_chunk > 1:
        take(1, 1)
    wait_all(s_copies, 0)
    assemble_sub(0)
    wait_all(x_copies, 0)
    assemble_col(0)
    for q in range(2, n_chunk):
        take(1, q)

    p_copies = []
    for m, ref in enumerate((gen_ref, int_ref)):
        for e in range(1, n_col):
            p_copies.append(
                remote(
                    ref,
                    partx.at[m, e - 1],
                    p_send.at[m, e - 1],
                    p_recv.at[m, e - 1],
                    to_col(e),
                )
            )
        for e in range(1, n_sub):
            p_copies.append(
                remote(
                    ref,
                    parts.at[m, e - 1],
                    p_send.at[m, n_col - 1 + e - 1],
                    p_recv.at[m, n_col - 1 + e - 1],
                    to_sub(e),
                )
            )
    assemble_own(1)
    wait_all(s_copies, 1)
    assemble_sub(1)
    wait_all(x_copies, 1)
    assemble_col(1)

    tall = min(256, height)
    wide = min(256, width)

    def multiply(write):
        def one(step, carry):
            rows = pl.ds(pl.multiple_of(step * tall, tall), tall)
            for c in range(width // wide):
                cols = pl.ds(c * wide, wide)
                total = None
                for k in range(n_col):
                    depth = pl.ds(k * width, width)
                    for m in range(2):
                        a_hi = left[m][0][k, rows, :]
                        a_lo = left[m][1][k, rows, :]
                        b_hi = right[1 - m][0][depth, cols]
                        b_lo = right[1 - m][1][depth, cols]
                        for a, b in ((a_hi, b_hi), (a_hi, b_lo), (a_lo, b_hi)):
                            term = jnp.dot(a, b, preferred_element_type=jnp.float32)
                            total = term if total is None else total + term
                write(step, rows, c, cols, total)
            return carry

        lax.fori_loop(0, height // tall, one, 0)

    def write_product(step, rows, c, cols, total):
        for r in range(tall // TR):
            for t in range(wide // TC):
                index = (step * (tall // TR) + r) * ct + c * (wide // TC) + t
                product[index] = total[r * TR : (r + 1) * TR, t * TC : (t + 1) * TC]

    multiply(write_product)

    for d in distances:
        target = lax.rem(me + d, n_chan)

        def put_back(k, carry, target=target, d=d):
            back_send[(d - 1) * cap + k] = product[smeta_own[target, 0, tiles + k]]
            return carry

        lax.fori_loop(0, cap, put_back, 0, unroll=min(cap, 4))

    def keep_back(k, carry):
        back_recv[me * cap + k] = product[smeta_own[me, 0, tiles + k]]
        return carry

    lax.fori_loop(0, cap, keep_back, 0, unroll=min(cap, 4))
    back_copies = [
        remote(
            back_send.at[pl.ds((d - 1) * cap, cap)],
            back_recv.at[pl.ds(me * cap, cap)],
            b_send.at[d - 1],
            b_recv.at[d - 1],
            to_chan(d),
        )
        for d in distances
    ]

    def place(m, read, in_left, in_right):
        def one_row(r, carry):
            rows = pl.ds(pl.multiple_of(r * TR, TR), TR)
            for t in range(ct):
                value = read(rows, pl.ds(t * TC, TC))
                if in_left is not None:
                    put_left(0, m, in_left, rows, t, value)
                if in_right is not None:
                    put_right(m, in_right, r, t, value)
            return carry

        lax.fori_loop(0, rt, one_row, 0)

    for m, ref in enumerate((gen_ref, int_ref)):
        place(m, lambda rows, cols, ref=ref: ref[rows, cols], my_col, my_sub)
    for copy in p_copies:
        copy.wait_recv()
    for m in range(2):
        for e in range(1, n_sub):
            place(
                m,
                lambda rows, cols, m=m, e=e: parts[m, e - 1, rows, cols],
                None,
                lax.rem(my_sub + n_sub - e, n_sub),
            )
        for e in range(1, n_col):
            place(
                m,
                lambda rows, cols, m=m, e=e: partx[m, e - 1, rows, cols],
                lax.rem(my_col + n_col - e, n_col),
                None,
            )

    def write_particle(step, rows, c, cols, total):
        particle[rows, cols] = total

    multiply(write_particle)

    for copy in back_copies:
        copy.wait_recv()

    def finish(r, carry):
        rows = pl.ds(pl.multiple_of(r * TR, TR), TR)
        for t in range(ct):
            cols = pl.ds(t * TC, TC)
            returned = back_recv[ret_ref[r * ct + t]]
            out_ref[rows, cols] = live_of(r, t) * (particle[rows, cols] - returned)
        return carry

    lax.fori_loop(0, rt, finish, 0)
    for copy in started:
        copy.wait_send()


def shards(
    generator,
    interaction,
    occupations,
    pair_orbits,
    cross_orbits,
    pair_sizes,
    cross_sizes,
    cross_target,
):
    height, width = generator.shape[1:]
    n_chan, n_col, n_sub = (lax.axis_size(axis) for axis in ("chan", "col", "sub"))
    rt, ct = height // TR, width // TC
    tiles = rt * ct
    cap = 2 * tiles // n_chan
    chunk = min(cap, 8)
    states = pair_orbits.shape[2]

    targets = cross_target[0].reshape(-1)
    owner = targets // tiles
    slot = targets % tiles
    index = jnp.arange(tiles, dtype=jnp.int32)
    same = (owner[:, None] == owner[None, :]) & (index[None, :] < index[:, None])
    rank = jnp.sum(same.astype(jnp.int32), axis=1)
    position = owner * cap + rank
    taken = position[None, :] == jnp.arange(n_chan * cap, dtype=jnp.int32)[:, None]
    pack_index = jnp.sum(jnp.where(taken, index[None, :], 0), axis=1)
    slot_map = jnp.sum(jnp.where(taken, slot[None, :], 0), axis=1)
    lands = targets[None, :] == jnp.arange(n_chan * tiles, dtype=jnp.int32)[:, None]
    label = lax.axis_index("chan") * cap + rank
    inverse = jnp.sum(jnp.where(lands, label[None, :], 0), axis=1)
    lanes = -(-(tiles + cap) // LANES) * LANES
    meta = jnp.concatenate(
        [
            inverse.reshape(n_chan, 1, tiles),
            slot_map.reshape(n_chan, 1, cap),
            jnp.zeros((n_chan, 1, lanes - tiles - cap), jnp.int32),
        ],
        axis=2,
    )
    sizes = jnp.stack([pair_sizes[0], cross_sizes[0]])
    filled = occupations.astype(jnp.float32)

    f32, bf16, i32 = jnp.float32, jnp.bfloat16, jnp.int32
    vmem = pl.BlockSpec(memory_space=pltpu.VMEM)
    smem = pl.BlockSpec(memory_space=pltpu.SMEM)
    dma = pltpu.SemaphoreType.DMA
    n_chunk = cap // chunk
    slots = n_chan * cap
    meta_row = (n_chan, 1, lanes)
    scratch = [
        pltpu.VMEM((tiles, TR, TC), f32),
        pltpu.VMEM((tiles, TR, TC), f32),
        pltpu.VMEM((slots - cap, TR, TC), f32),
        pltpu.VMEM((slots - cap, TR, TC), f32),
        pltpu.VMEM((slots, TR, TC), f32),
        pltpu.VMEM((slots, TR, TC), f32),
        pltpu.VMEM((n_col - 1, slots, TR, TC), f32),
        pltpu.VMEM((n_col - 1, slots, TR, TC), f32),
        pltpu.VMEM((n_sub - 1, slots, TR, TC), f32),
        pltpu.VMEM((n_sub - 1, slots, TR, TC), f32),
        pltpu.VMEM(meta_row, i32),
        pltpu.VMEM((n_col - 1,) + meta_row, i32),
        pltpu.VMEM((n_sub - 1,) + meta_row, i32),
        pltpu.SMEM(meta_row, i32),
        pltpu.SMEM((n_col - 1,) + meta_row, i32),
        pltpu.SMEM((n_sub - 1,) + meta_row, i32),
    ]
    scratch += [pltpu.VMEM((n_col, height, width), bf16)] * 4
    scratch += [pltpu.VMEM((n_sub * height, width), bf16)] * 4
    scratch += [
        pltpu.VMEM((tiles, TR, TC), f32),
        pltpu.VMEM((slots - cap, TR, TC), f32),
        pltpu.VMEM((slots, TR, TC), f32),
        pltpu.VMEM((2, n_col - 1, height, width), f32),
        pltpu.VMEM((2, n_sub - 1, height, width), f32),
        pltpu.VMEM((height, width), f32),
        pltpu.VMEM((2, states // TC, 8, TC), f32),
        dma((2, n_chunk, n_chan - 1)),
        dma((2, n_chunk, n_chan - 1)),
        dma((2, n_chunk, n_chan, n_col - 1)),
        dma((2, n_chunk, n_chan, n_col - 1)),
        dma((2, n_chunk, n_chan, n_sub - 1)),
        dma((2, n_chunk, n_chan, n_sub - 1)),
        dma((n_chan + n_col + n_sub - 3,)),
        dma((n_chan + n_col + n_sub - 3,)),
        dma((3,)),
        dma((n_chan - 1,)),
        dma((n_chan - 1,)),
        dma((2, n_col + n_sub - 2)),
        dma((2, n_col + n_sub - 2)),
    ]
    static = (n_chan, n_col, n_sub, height, width, cap, chunk)
    result = pl.pallas_call(
        functools.partial(kernel, static),
        out_shape=jax.ShapeDtypeStruct((height, width), f32),
        in_specs=[vmem, vmem, vmem, vmem, smem, smem, smem, smem, vmem],
        out_specs=vmem,
        scratch_shapes=scratch,
        compiler_params=pltpu.CompilerParams(
            collective_id=0, has_side_effects=True, vmem_limit_bytes=VMEM_LIMIT
        ),
        name="commutator",
    )(
        generator[0],
        interaction[0],
        pair_orbits[0],
        cross_orbits[0],
        filled,
        sizes,
        pack_index,
        position,
        meta,
    )
    return result[None]


def solution(mesh):
    return jax.shard_map(
        shards,
        mesh=mesh,
        in_specs=(
            P(("grp", "chan"), "sub", "col"),
            P(("grp", "chan"), "sub", "col"),
            P(),
            P("chan", None, None),
            P("chan", None, None),
            P("chan"),
            P("chan"),
            P("chan", "sub", "col"),
        ),
        out_specs=P(("grp", "chan"), "sub", "col"),
        check_vma=False,
    )
```

time: 311 us -> 174 us (0.56)
  the two profiles are of different devices: /device:TPU:17 before, /device:TPU:0 now
where the time goes in v1:
time: 174 us
  Pallas kernels  166 us (95%)
  local copies, waits for them, and re-layouts  3.75 us (2%)
  other arithmetic  2.76 us (2%)
    pallas_call x1, Pallas kernels, shards(): pl.pallas_call(functools.partial(kernel, static), out_shape=jax.ShapeDtyp...  166 us

profile of v1, /device:TPU:0, one launch (start us, length us, event | category | flops | bytes accessed | tf_op | source)
XLA Modules:
  0.0 174.0 jit_solution(11425626277527818599)
XLA Ops:
  1.3 0.6 pad_add_fusion.size_ref
  1.9 0.0 copy-start.2
  1.9 0.0 copy-start.1
  1.9 0.1 pad.2.clone
  2.0 0.6 copy-done.2
  2.6 0.6 convert_element_type.6.filled_ref
  3.2 0.0 copy-done.1
  3.2 0.1 copy.13
  3.2 0.1 reshape_squeeze.3
  3.3 0.2 convert_reduce_fusion
  3.5 0.0 copy-start
  3.5 0.1 select_reduce_fusion
  3.6 0.5 copy-done
  4.1 0.6 select_reduce_fusion.1
  4.8 0.1 reshape.100
  4.8 0.1 reshape.101
  4.9 0.7 add_add_fusion.meta_ref
  5.6 166.2 %commutator.1 = f32[512,512]{1,0:T(8,128)} custom-call(f32[512,512]{1,0:T(8,128)} %bitcast.7, f32[512,512]{1,0:T(8,128)} %bitcast.8, s32[2,1024]{1,0:T(2,128)} %bitcast.9, s32[2,1024]{1,0:T(2,128)} %bitcast.10, f32[160]{0:T(256)} %convert_element_type.6.filled_ref, s32[2]{0:T(128)} %pad_add_fusion.size_ref, s32[128]{0:T(128)} %get-tuple-element.6.pack_ref, ...), custom_call_target="tpu_custom_call" | custom-call | tf_op jit(solution)/shard_map/commutator/pallas_call | solution.py:595
  171.8 2.3 %copy.18 = f32[1,512,512]{2,1,0:T(8,128)} copy(f32[1,512,512]{2,1,0:T(8,128)} %bitcast.6) | data formatting | bytes 2097152
  (3 shorter events, 0.0 us)
Async XLA Ops:
  1.9 0.7 copy-start.2
  1.9 1.3 copy-start.1
  3.5 0.6 copy-start

commit v2 on v1

v2 whole, which is shorter than its diff:
```python
import functools

import jax
import jax.numpy as jnp
from jax import lax
from jax.experimental import pallas as pl
from jax.experimental.pallas import tpu as pltpu
from jax.sharding import PartitionSpec as P

TR = 32
TC = 128
LANES = 128
MESH = pl.DeviceIdType.MESH
VMEM_LIMIT = 60 * 1024 * 1024
ROWS = 8
SLICES = TR // ROWS
LEAD = 2


def split(value):
    high = value.astype(jnp.bfloat16)
    low = (value - high.astype(jnp.float32)).astype(jnp.bfloat16)
    return high, low


def outer_first(count):
    order = []
    for edge in range((count + 1) // 2):
        order += [edge] if edge == count - 1 - edge else [edge, count - 1 - edge]
    return order, count // 2


def kernel(sizes, *refs):
    n_chan, n_col, n_sub, height, width, cap = sizes
    refs = list(refs)

    def grab(count):
        taken = refs[:count]
        del refs[:count]
        return taken

    gen_ref, int_ref, pair_orb_ref, cross_orb_ref, filled_ref = grab(5)
    size_ref, pack_ref, ret_ref, meta_ref, out_ref = grab(5)
    tiled = grab(2)
    sent = grab(2)
    raw = (grab(SLICES), grab(SLICES))
    whole = grab(2)
    from_col = grab(2)
    from_sub = grab(2)
    meta_own, smeta = grab(2)
    left = (grab(2), grab(2))
    right = (grab(2), grab(2))
    product, back_send, back_recv, partx, parts, particle, weights = grab(7)
    z_send, z_recv, x_send, x_recv, s_send, s_recv = grab(6)
    m_send, m_recv, local_sem, b_send, b_recv, p_send, p_recv = grab(7)

    rt, ct = height // TR, width // TC
    tiles = rt * ct
    me = lax.axis_index("chan")
    my_col = lax.axis_index("col")
    my_sub = lax.axis_index("sub")

    def to_col(step):
        return {"col": lax.rem(my_col + step, n_col)}

    def to_sub(step):
        return {"sub": lax.rem(my_sub + step, n_sub)}

    order, outer_count = outer_first(n_chan)
    upper = me // max(n_chan // 2, 1)
    peers = [upper * t + (1 - upper) * (n_chan - 1 - t) for t in order]

    barrier = pltpu.get_barrier_semaphore()
    for d in range(1, n_chan):
        pl.semaphore_signal(
            barrier, inc=1, device_id={"chan": lax.rem(me + d, n_chan)}, device_id_type=MESH
        )
    for d in range(1, n_col):
        pl.semaphore_signal(barrier, inc=1, device_id=to_col(d), device_id_type=MESH)
    for d in range(1, n_sub):
        pl.semaphore_signal(barrier, inc=1, device_id=to_sub(d), device_id_type=MESH)

    limit = size_ref[0]
    row_in = lax.broadcasted_iota(jnp.int32, (TR, TC), 0) + my_sub * height
    col_in = lax.broadcasted_iota(jnp.int32, (TR, TC), 1) + my_col * width

    def live_of(r, t):
        keep = (row_in + r * TR < limit) & (col_in + t * TC < limit)
        return keep.astype(jnp.float32)

    own_meta = pltpu.make_async_copy(meta_ref.at[me], meta_own.at[me], local_sem.at[0])
    own_meta.start()

    def to_tiles(r, carry):
        rows = pl.ds(pl.multiple_of(r * TR, TR), TR)
        for t in range(ct):
            keep = live_of(r, t)
            cols = pl.ds(t * TC, TC)
            tiled[0][r * ct + t] = gen_ref[rows, cols] * keep
            tiled[1][r * ct + t] = int_ref[rows, cols] * keep
        return carry

    lax.fori_loop(0, rt, to_tiles, 0)

    def pack_one(m):
        def put(k, carry):
            value = tiled[m][pack_ref[k]]
            for q in range(SLICES):
                sent[m][q, k] = value[q * ROWS : (q + 1) * ROWS]
            return carry

        lax.fori_loop(0, n_chan * cap, put, 0, unroll=8)

        def keep_own(k, carry):
            value = tiled[m][pack_ref[me * cap + k]]
            for q in range(SLICES):
                raw[m][q][me * cap + k] = value[q * ROWS : (q + 1) * ROWS]
            return carry

        lax.fori_loop(0, cap, keep_own, 0, unroll=min(cap, 4))

    pack_one(0)
    pl.semaphore_wait(barrier, n_chan + n_col + n_sub - 3)

    def remote(src, dst, ssem, rsem, device):
        return pltpu.make_async_remote_copy(
            src_ref=src,
            dst_ref=dst,
            send_sem=ssem,
            recv_sem=rsem,
            device_id=device,
            device_id_type=MESH,
        )

    def others(peer_list, act):
        for peer in peer_list:

            @pl.when(peer != me)
            def _(peer=peer):
                act(peer)

    def meta_copy(peer, source):
        return remote(
            meta_ref.at[peer],
            meta_own.at[source],
            m_send.at[peer],
            m_recv.at[source],
            {"chan": peer},
        )

    def z_copy(m, q, peer, source):
        return remote(
            sent[m].at[q, pl.ds(peer * cap, cap)],
            raw[m][q].at[pl.ds(source * cap, cap)],
            z_send.at[m, q, peer],
            z_recv.at[m, q, source],
            {"chan": peer},
        )

    def back_copy(peer, source):
        return remote(
            back_send.at[pl.ds(peer * cap, cap)],
            back_recv.at[pl.ds(source * cap, cap)],
            b_send.at[peer],
            b_recv.at[source],
            {"chan": peer},
        )

    stages = [(m, q) for m in range(2) for q in range(SLICES)]
    outer, inner = peers[:outer_count], peers[outer_count:]

    def send_steps(first, last):
        for step in range(first, last):
            if step < len(stages):
                others(outer, lambda p, s=stages[step]: z_copy(*s, p, me).start())
            if step >= LEAD:
                others(inner, lambda p, s=stages[step - LEAD]: z_copy(*s, p, me).start())

    others(peers, lambda p: meta_copy(p, me).start())
    send_steps(0, SLICES)

    started = []

    def start(copy):
        copy.start()
        started.append(copy)
        return copy

    p_copies = ([], [])

    def send_particle(m):
        ref = (gen_ref, int_ref)[m]
        for e in range(1, n_col):
            p_copies[m].append(
                start(
                    remote(
                        ref,
                        partx.at[m, e - 1],
                        p_send.at[m, e - 1],
                        p_recv.at[m, e - 1],
                        to_col(e),
                    )
                )
            )
        for e in range(1, n_sub):
            p_copies[m].append(
                start(
                    remote(
                        ref,
                        parts.at[m, e - 1],
                        p_send.at[m, n_col - 1 + e - 1],
                        p_recv.at[m, n_col - 1 + e - 1],
                        to_sub(e),
                    )
                )
            )

    send_particle(0)
    pack_one(1)
    send_steps(SLICES, len(stages) + LEAD)

    states = pair_orb_ref.shape[1]

    def look_up(orbit, found):
        value = filled_ref[orbit]
        pair_found, cross_found = found
        pair_found = pair_found + jnp.where(pair_orb_ref[...] == orbit, value, 0.0)
        cross_found = cross_found + jnp.where(cross_orb_ref[...] == orbit, value, 0.0)
        return pair_found, cross_found

    zero = jnp.zeros((2, states), jnp.float32)
    pair_found, cross_found = lax.fori_loop(0, filled_ref.shape[0], look_up, (zero, zero))
    state_id = lax.broadcasted_iota(jnp.int32, (1, states), 1)
    pair_weight = (1.0 - pair_found[0:1] - pair_found[1:2]) * (state_id < limit).astype(jnp.float32)
    cross_weight = (cross_found[0:1] - cross_found[1:2]) * (state_id < size_ref[1]).astype(
        jnp.float32
    )
    for g in range(states // TC):
        weights[0, g] = jnp.broadcast_to(pair_weight[:, g * TC : (g + 1) * TC], (8, TC))
        weights[1, g] = jnp.broadcast_to(cross_weight[:, g * TC : (g + 1) * TC], (8, TC))

    own_meta.wait()
    others(peers, lambda p: meta_copy(p, p).wait_recv())
    to_scalar = pltpu.make_async_copy(meta_own, smeta, local_sem.at[0])
    to_scalar.start()
    to_scalar.wait()

    x_copies, s_copies = {}, {}

    def take(m, q):
        others(peers, lambda p: z_copy(m, q, p, p).wait_recv())

        def one(j, carry):
            where = smeta[0, 0, j]
            for source in range(1, n_chan):
                where = where + smeta[source, 0, j]
            whole[m][q, j] = raw[m][q][where]
            return carry

        lax.fori_loop(0, tiles, one, 0, unroll=8)
        for e in range(1, n_col):
            x_copies[m, q, e] = start(
                remote(
                    whole[m].at[q],
                    from_col[m].at[e - 1, q],
                    x_send.at[m, q, e - 1],
                    x_recv.at[m, q, e - 1],
                    to_col(e),
                )
            )
        for e in range(1, n_sub):
            s_copies[m, q, e] = start(
                remote(
                    whole[m].at[q],
                    from_sub[m].at[e - 1, q],
                    s_send.at[m, q, e - 1],
                    s_recv.at[m, q, e - 1],
                    to_sub(e),
                )
            )

    def put_left(which, m, block, rows, t, value):
        weight = weights[which, block * ct + t][0:1]
        signed = value * (weight if m == 0 else -weight)
        high, low = split(signed)
        cols = pl.ds(t * TC, TC)
        left[m][0][block, rows, cols] = high
        left[m][1][block, rows, cols] = low

    def put_right(m, block, r, t, value):
        rows = pl.ds(pl.multiple_of(block * height + r * TR, TR), TR)
        high, low = split(value)
        cols = pl.ds(t * TC, TC)
        right[m][0][rows, cols] = high
        right[m][1][rows, cols] = low

    def place(which, m, read, in_left, in_right):
        def one_row(r, carry):
            rows = pl.ds(pl.multiple_of(r * TR, TR), TR)
            for t in range(ct):
                value = read(r, t, rows)
                if in_left is not None:
                    put_left(which, m, in_left, rows, t, value)
                if in_right is not None:
                    put_right(m, in_right, r, t, value)
            return carry

        lax.fori_loop(0, rt, one_row, 0)

    def joined(ref, r, t, *lead):
        parts_of = [ref[(*lead, q, r * ct + t)] for q in range(SLICES)]
        return jnp.concatenate(parts_of, axis=0)

    def col_block(e):
        return lax.rem(my_col + n_col - e, n_col)

    def sub_block(e):
        return lax.rem(my_sub + n_sub - e, n_sub)

    def settle(m):
        place(1, m, lambda r, t, rows: joined(whole[m], r, t), my_col, my_sub)
        for e in range(1, n_sub):
            for q in range(SLICES):
                s_copies[m, q, e].wait_recv()
            place(1, m, lambda r, t, rows: joined(from_sub[m], r, t, e - 1), None, sub_block(e))
        for e in range(1, n_col):
            for q in range(SLICES):
                x_copies[m, q, e].wait_recv()
            place(1, m, lambda r, t, rows: joined(from_col[m], r, t, e - 1), col_block(e), None)

    for q in range(SLICES):
        take(0, q)
    for q in range(SLICES - 1):
        take(1, q)
    settle(0)
    take(1, SLICES - 1)
    send_particle(1)
    settle(1)

    tall = min(256, height)
    wide = min(256, width)

    def multiply(write):
        def one(step, carry):
            rows = pl.ds(pl.multiple_of(step * tall, tall), tall)
            for c in range(width // wide):
                cols = pl.ds(c * wide, wide)
                total = None
                for k in range(n_col):
                    depth = pl.ds(k * width, width)
                    for m in range(2):
                        a_hi = left[m][0][k, rows, :]
                        a_lo = left[m][1][k, rows, :]
                        b_hi = right[1 - m][0][depth, cols]
                        b_lo = right[1 - m][1][depth, cols]
                        for a, b in ((a_hi, b_hi), (a_hi, b_lo), (a_lo, b_hi)):
                            term = jnp.dot(a, b, preferred_element_type=jnp.float32)
                            total = term if total is None else total + term
                write(step, rows, c, cols, total)
            return carry

        lax.fori_loop(0, height // tall, one, 0)

    def write_product(step, rows, c, cols, total):
        for r in range(tall // TR):
            for t in range(wide // TC):
                index = (step * (tall // TR) + r) * ct + c * (wide // TC) + t
                product[index] = total[r * TR : (r + 1) * TR, t * TC : (t + 1) * TC]

    multiply(write_product)

    def send_back(peer):
        def put_back(k, carry):
            back_send[peer * cap + k] = product[smeta[peer, 0, tiles + k]]
            return carry

        lax.fori_loop(0, cap, put_back, 0, unroll=min(cap, 8))

    others(peers, send_back)

    def keep_back(k, carry):
        back_recv[me * cap + k] = product[smeta[me, 0, tiles + k]]
        return carry

    lax.fori_loop(0, cap, keep_back, 0, unroll=min(cap, 8))
    others(peers, lambda p: back_copy(p, me).start())

    for m, ref in enumerate((gen_ref, int_ref)):
        place(
            0, m, lambda r, t, rows, ref=ref: ref[rows, pl.ds(t * TC, TC)], my_col, my_sub
        )
    for m in range(2):
        for copy in p_copies[m]:
            copy.wait_recv()
        for e in range(1, n_sub):
            place(
                0,
                m,
                lambda r, t, rows: parts[m, e - 1, rows, pl.ds(t * TC, TC)],
                None,
                sub_block(e),
            )
        for e in range(1, n_col):
            place(
                0,
                m,
                lambda r, t, rows: partx[m, e - 1, rows, pl.ds(t * TC, TC)],
                col_block(e),
                None,
            )

    def write_particle(step, rows, c, cols, total):
        particle[rows, cols] = total

    multiply(write_particle)
    others(peers, lambda p: back_copy(p, p).wait_recv())

    def finish(r, carry):
        rows = pl.ds(pl.multiple_of(r * TR, TR), TR)
        for t in range(ct):
            cols = pl.ds(t * TC, TC)
            returned = back_recv[ret_ref[r * ct + t]]
            out_ref[rows, cols] = live_of(r, t) * (particle[rows, cols] - returned)
        return carry

    lax.fori_loop(0, rt, finish, 0)
    others(peers, lambda p: meta_copy(p, me).wait_send())
    for m, q in stages:
        others(peers, lambda p: z_copy(m, q, p, me).wait_send())
    others(peers, lambda p: back_copy(p, me).wait_send())
    for copy in started:
        copy.wait_send()


def shards(
    generator,
    interaction,
    occupations,
    pair_orbits,
    cross_orbits,
    pair_sizes,
    cross_sizes,
    cross_target,
):
    height, width = generator.shape[1:]
    n_chan, n_col, n_sub = (lax.axis_size(axis) for axis in ("chan", "col", "sub"))
    rt, ct = height // TR, width // TC
    tiles = rt * ct
    cap = 2 * tiles // n_chan
    states = pair_orbits.shape[2]

    targets = cross_target[0].reshape(-1)
    owner = targets // tiles
    slot = targets % tiles
    index = jnp.arange(tiles, dtype=jnp.int32)
    same = (owner[:, None] == owner[None, :]) & (index[None, :] < index[:, None])
    rank = jnp.sum(same.astype(jnp.int32), axis=1)
    position = owner * cap + rank
    taken = position[None, :] == jnp.arange(n_chan * cap, dtype=jnp.int32)[:, None]
    pack_index = jnp.sum(jnp.where(taken, index[None, :], 0), axis=1)
    slot_map = jnp.sum(jnp.where(taken, slot[None, :], 0), axis=1)
    lands = targets[None, :] == jnp.arange(n_chan * tiles, dtype=jnp.int32)[:, None]
    label = lax.axis_index("chan") * cap + rank
    inverse = jnp.sum(jnp.where(lands, label[None, :], 0), axis=1)
    lanes = -(-(tiles + cap) // LANES) * LANES
    meta = jnp.concatenate(
        [
            inverse.reshape(n_chan, 1, tiles),
            slot_map.reshape(n_chan, 1, cap),
            jnp.zeros((n_chan, 1, lanes - tiles - cap), jnp.int32),
        ],
        axis=2,
    )
    sizes = jnp.stack([pair_sizes[0], cross_sizes[0]])
    filled = occupations.astype(jnp.float32)

    f32, bf16, i32 = jnp.float32, jnp.bfloat16, jnp.int32
    vmem = pl.BlockSpec(memory_space=pltpu.VMEM)
    smem = pl.BlockSpec(memory_space=pltpu.SMEM)
    dma = pltpu.SemaphoreType.DMA
    slots = n_chan * cap
    meta_row = (n_chan, 1, lanes)
    slice_of = (ROWS, TC)
    scratch = [pltpu.VMEM((tiles, TR, TC), f32)] * 2
    scratch += [pltpu.VMEM((SLICES, slots) + slice_of, f32)] * 2
    scratch += [pltpu.VMEM((slots,) + slice_of, f32)] * (2 * SLICES)
    scratch += [pltpu.VMEM((SLICES, tiles) + slice_of, f32)] * 2
    scratch += [pltpu.VMEM((n_col - 1, SLICES, tiles) + slice_of, f32)] * 2
    scratch += [pltpu.VMEM((n_sub - 1, SLICES, tiles) + slice_of, f32)] * 2
    scratch += [pltpu.VMEM(meta_row, i32), pltpu.SMEM(meta_row, i32)]
    scratch += [pltpu.VMEM((n_col, height, width), bf16)] * 4
    scratch += [pltpu.VMEM((n_sub * height, width), bf16)] * 4
    scratch += [
        pltpu.VMEM((tiles, TR, TC), f32),
        pltpu.VMEM((slots, TR, TC), f32),
        pltpu.VMEM((slots, TR, TC), f32),
        pltpu.VMEM((2, n_col - 1, height, width), f32),
        pltpu.VMEM((2, n_sub - 1, height, width), f32),
        pltpu.VMEM((height, width), f32),
        pltpu.VMEM((2, states // TC, 8, TC), f32),
    ]
    scratch += [dma((2, SLICES, n_chan))] * 2
    scratch += [dma((2, SLICES, n_col - 1))] * 2
    scratch += [dma((2, SLICES, n_sub - 1))] * 2
    scratch += [dma((n_chan,))] * 2
    scratch += [dma((1,))]
    scratch += [dma((n_chan,))] * 2
    scratch += [dma((2, n_col + n_sub - 2))] * 2
    static = (n_chan, n_col, n_sub, height, width, cap)
    result = pl.pallas_call(
        functools.partial(kernel, static),
        out_shape=jax.ShapeDtypeStruct((height, width), f32),
        in_specs=[vmem, vmem, vmem, vmem, smem, smem, smem, smem, vmem],
        out_specs=vmem,
        scratch_shapes=scratch,
        compiler_params=pltpu.CompilerParams(
            collective_id=0, has_side_effects=True, vmem_limit_bytes=VMEM_LIMIT
        ),
        name="commutator",
    )(
        generator[0],
        interaction[0],
        pair_orbits[0],
        cross_orbits[0],
        filled,
        sizes,
        pack_index,
        position,
        meta,
    )
    return result[None]


def solution(mesh):
    return jax.shard_map(
        shards,
        mesh=mesh,
        in_specs=(
            P(("grp", "chan"), "sub", "col"),
            P(("grp", "chan"), "sub", "col"),
            P(),
            P("chan", None, None),
            P("chan", None, None),
            P("chan"),
            P("chan"),
            P("chan", "sub", "col"),
        ),
        out_specs=P(("grp", "chan"), "sub", "col"),
        check_vma=False,
    )
```

time: 174 us -> 155 us (0.89)
  the two profiles are of different devices: /device:TPU:0 before, /device:TPU:17 now
where the time goes in v2:
time: 155 us
  Pallas kernels  147 us (95%)
  local copies, waits for them, and re-layouts  3.75 us (2%)
  other arithmetic  2.76 us (2%)
    pallas_call x1, Pallas kernels, shards(): pl.pallas_call(functools.partial(kernel, static), out_shape=jax.ShapeDtyp...  147 us
    unnamed x8, local copies, waits for them, and re-layouts  3.42 us

profile of v2, /device:TPU:17, one launch (start us, length us, event | category | flops | bytes accessed | tf_op | source)
XLA Modules:
  0.0 155.2 jit_solution(15091884553148695575)
XLA Ops:
  1.3 0.6 pad_add_fusion.refs_5_
  1.9 0.0 copy-start.2
  1.9 0.0 copy-start.1
  1.9 0.1 pad.2.clone
  2.0 0.6 copy-done.2
  2.6 0.6 convert_element_type.6.refs_4_
  3.2 0.0 copy-done.1
  3.2 0.1 copy.13
  3.2 0.1 reshape_squeeze.3
  3.3 0.2 convert_reduce_fusion
  3.5 0.0 copy-start
  3.5 0.1 select_reduce_fusion
  3.6 0.5 copy-done
  4.1 0.6 select_reduce_fusion.1
  4.8 0.1 reshape.100
  4.8 0.1 reshape.101
  4.9 0.7 add_add_fusion.refs_8_
  5.6 147.3 %commutator.1 = f32[512,512]{1,0:T(8,128)} custom-call(f32[512,512]{1,0:T(8,128)} %bitcast.7, f32[512,512]{1,0:T(8,128)} %bitcast.8, s32[2,1024]{1,0:T(2,128)} %bitcast.9, s32[2,1024]{1,0:T(2,128)} %bitcast.10, f32[160]{0:T(256)} %convert_element_type.6.refs_4_, s32[2]{0:T(128)} %pad_add_fusion.refs_5_, s32[128]{0:T(128)} %get-tuple-element.6.refs_6_, ...), custom_call_target="tpu_custom_call" | custom-call | tf_op jit(solution)/shard_map/commutator/pallas_call | solution.py:510
  152.9 2.3 %copy.18 = f32[1,512,512]{2,1,0:T(8,128)} copy(f32[1,512,512]{2,1,0:T(8,128)} %bitcast.6) | data formatting | bytes 2097152
  (3 shorter events, 0.0 us)
Async XLA Ops:
  1.9 0.7 copy-start.2
  1.9 1.3 copy-start.1
  3.5 0.6 copy-start

commit v3 on v2

--- a/solution.py
+++ b/solution.py
@@ -11,7 +11,7 @@
 TC = 128
 LANES = 128
 MESH = pl.DeviceIdType.MESH
-VMEM_LIMIT = 60 * 1024 * 1024
+VMEM_LIMIT = 44 * 1024 * 1024
 ROWS = 8
 SLICES = TR // ROWS
 LEAD = 2
@@ -40,14 +40,14 @@
         return taken
 
     gen_ref, int_ref, pair_orb_ref, cross_orb_ref, filled_ref = grab(5)
-    size_ref, pack_ref, ret_ref, meta_ref, out_ref = grab(5)
+    pair_size_ref, cross_size_ref, pack_ref, ret_ref, target_ref, out_ref = grab(6)
     tiled = grab(2)
     sent = grab(2)
     raw = (grab(SLICES), grab(SLICES))
     whole = grab(2)
     from_col = grab(2)
     from_sub = grab(2)
-    meta_own, smeta = grab(2)
+    meta_ref, meta_own, smeta = grab(3)
     left = (grab(2), grab(2))
     right = (grab(2), grab(2))
     product, back_send, back_recv, partx, parts, particle, weights = grab(7)
@@ -80,16 +80,13 @@
     for d in range(1, n_sub):
         pl.semaphore_signal(barrier, inc=1, device_id=to_sub(d), device_id_type=MESH)
 
-    limit = size_ref[0]
+    limit = pair_size_ref[0]
     row_in = lax.broadcasted_iota(jnp.int32, (TR, TC), 0) + my_sub * height
     col_in = lax.broadcasted_iota(jnp.int32, (TR, TC), 1) + my_col * width
 
     def live_of(r, t):
         keep = (row_in + r * TR < limit) & (col_in + t * TC < limit)
         return keep.astype(jnp.float32)
-
-    own_meta = pltpu.make_async_copy(meta_ref.at[me], meta_own.at[me], local_sem.at[0])
-    own_meta.start()
 
     def to_tiles(r, carry):
         rows = pl.ds(pl.multiple_of(r * TR, TR), TR)
@@ -119,6 +116,21 @@
 
         lax.fori_loop(0, cap, keep_own, 0, unroll=min(cap, 4))
 
+    meta_shape = (n_chan, meta_ref.shape[2])
+    lane = lax.broadcasted_iota(jnp.int32, meta_shape, 1)
+    to = lax.broadcasted_iota(jnp.int32, meta_shape, 0)
+    land_id = jnp.where(lane < tiles, to * tiles + lane, -1)
+    slot_id = jnp.where((lane >= tiles) & (lane < tiles + cap), to * cap + lane - tiles, -1)
+
+    def fill_meta(i, rows):
+        target, place_of = target_ref[i], ret_ref[i]
+        owner = lax.div(target, tiles)
+        rows = jnp.where(land_id == target, (me - owner) * cap + place_of, rows)
+        return jnp.where(slot_id == place_of, target - owner * tiles, rows)
+
+    meta_rows = lax.fori_loop(0, tiles, fill_meta, jnp.zeros(meta_shape, jnp.int32), unroll=4)
+    for d in range(n_chan):
+        meta_ref[d] = meta_rows[d : d + 1]
     pack_one(0)
     pl.semaphore_wait(barrier, n_chan + n_col + n_sub - 3)
 
@@ -176,6 +188,8 @@
             if step >= LEAD:
                 others(inner, lambda p, s=stages[step - LEAD]: z_copy(*s, p, me).start())
 
+    own_meta = pltpu.make_async_copy(meta_ref.at[me], meta_own.at[me], local_sem.at[0])
+    own_meta.start()
     others(peers, lambda p: meta_copy(p, me).start())
     send_steps(0, SLICES)
 
@@ -222,7 +236,7 @@
     states = pair_orb_ref.shape[1]
 
     def look_up(orbit, found):
-        value = filled_ref[orbit]
+        value = filled_ref[orbit].astype(jnp.float32)
         pair_found, cross_found = found
         pair_found = pair_found + jnp.where(pair_orb_ref[...] == orbit, value, 0.0)
         cross_found = cross_found + jnp.where(cross_orb_ref[...] == orbit, value, 0.0)
@@ -232,7 +246,7 @@
     pair_found, cross_found = lax.fori_loop(0, filled_ref.shape[0], look_up, (zero, zero))
     state_id = lax.broadcasted_iota(jnp.int32, (1, states), 1)
     pair_weight = (1.0 - pair_found[0:1] - pair_found[1:2]) * (state_id < limit).astype(jnp.float32)
-    cross_weight = (cross_found[0:1] - cross_found[1:2]) * (state_id < size_ref[1]).astype(
+    cross_weight = (cross_found[0:1] - cross_found[1:2]) * (state_id < cross_size_ref[0]).astype(
         jnp.float32
     )
     for g in range(states // TC):
@@ -254,7 +268,7 @@
             where = smeta[0, 0, j]
             for source in range(1, n_chan):
                 where = where + smeta[source, 0, j]
-            whole[m][q, j] = raw[m][q][where]
+            whole[m][q, j] = raw[m][q][jnp.minimum(where, n_chan * cap - 1)]
             return carry
 
         lax.fori_loop(0, tiles, one, 0, unroll=8)
@@ -420,7 +434,7 @@
         for t in range(ct):
             cols = pl.ds(t * TC, TC)
             returned = back_recv[ret_ref[r * ct + t]]
-            out_ref[rows, cols] = live_of(r, t) * (particle[rows, cols] - returned)
+            out_ref[rows, cols] = particle[rows, cols] - returned
         return carry
 
     lax.fori_loop(0, rt, finish, 0)
@@ -451,29 +465,13 @@
 
     targets = cross_target[0].reshape(-1)
     owner = targets // tiles
-    slot = targets % tiles
     index = jnp.arange(tiles, dtype=jnp.int32)
     same = (owner[:, None] == owner[None, :]) & (index[None, :] < index[:, None])
     rank = jnp.sum(same.astype(jnp.int32), axis=1)
     position = owner * cap + rank
     taken = position[None, :] == jnp.arange(n_chan * cap, dtype=jnp.int32)[:, None]
     pack_index = jnp.sum(jnp.where(taken, index[None, :], 0), axis=1)
-    slot_map = jnp.sum(jnp.where(taken, slot[None, :], 0), axis=1)
-    lands = targets[None, :] == jnp.arange(n_chan * tiles, dtype=jnp.int32)[:, None]
-    label = lax.axis_index("chan") * cap + rank
-    inverse = jnp.sum(jnp.where(lands, label[None, :], 0), axis=1)
     lanes = -(-(tiles + cap) // LANES) * LANES
-    meta = jnp.concatenate(
-        [
-            inverse.reshape(n_chan, 1, tiles),
-            slot_map.reshape(n_chan, 1, cap),
-            jnp.zeros((n_chan, 1, lanes - tiles - cap), jnp.int32),
-        ],
-        axis=2,
-    )
-    sizes = jnp.stack([pair_sizes[0], cross_sizes[0]])
-    filled = occupations.astype(jnp.float32)
-
     f32, bf16, i32 = jnp.float32, jnp.bfloat16, jnp.int32
     vmem = pl.BlockSpec(memory_space=pltpu.VMEM)
     smem = pl.BlockSpec(memory_space=pltpu.SMEM)
@@ -487,7 +485,7 @@
     scratch += [pltpu.VMEM((SLICES, tiles) + slice_of, f32)] * 2
     scratch += [pltpu.VMEM((n_col - 1, SLICES, tiles) + slice_of, f32)] * 2
     scratch += [pltpu.VMEM((n_sub - 1, SLICES, tiles) + slice_of, f32)] * 2
-    scratch += [pltpu.VMEM(meta_row, i32), pltpu.SMEM(meta_row, i32)]
+    scratch += [pltpu.VMEM(meta_row, i32)] * 2 + [pltpu.SMEM(meta_row, i32)]
     scratch += [pltpu.VMEM((n_col, height, width), bf16)] * 4
     scratch += [pltpu.VMEM((n_sub * height, width), bf16)] * 4
     scratch += [
@@ -510,7 +508,7 @@
     result = pl.pallas_call(
         functools.partial(kernel, static),
         out_shape=jax.ShapeDtypeStruct((height, width), f32),
-        in_specs=[vmem, vmem, vmem, vmem, smem, smem, smem, smem, vmem],
+        in_specs=[vmem] * 4 + [smem] * 6,
         out_specs=vmem,
         scratch_shapes=scratch,
         compiler_params=pltpu.CompilerParams(
@@ -522,13 +520,17 @@
         interaction[0],
         pair_orbits[0],
         cross_orbits[0],
-        filled,
-        sizes,
+        occupations,
+        pair_sizes,
+        cross_sizes,
         pack_index,
         position,
-        meta,
+        targets,
     )
-    return result[None]
+    row_id = lax.axis_index("sub") * height + jnp.arange(height, dtype=jnp.int32)
+    col_id = lax.axis_index("col") * width + jnp.arange(width, dtype=jnp.int32)
+    live = (row_id < pair_sizes[0])[:, None] & (col_id < pair_sizes[0])[None, :]
+    return (live.astype(f32) * result)[None]
 
 
 def solution(mesh):

time: 155 us -> 152 us (0.981)
  Pallas kernels: 147 us -> 145 us
    pallas_call x1, Pallas kernels: 147 us -> 145 us  [shards(): pl.pallas_call(functools.partial(kernel, static), out_shape=jax.ShapeDtyp...]
    unnamed x8 -> x11, local copies, waits for them, and re-layouts: 3.42 us -> 3.87 us
where the time goes in v3:
time: 152 us; the launch traced here: 151 us
  Pallas kernels  145 us (95%)
  local copies, waits for them, and re-layouts  3.96 us (3%)
    pallas_call x1, Pallas kernels, shards(): pl.pallas_call(functools.partial(kernel, static), out_shape=jax.ShapeDtyp...  145 us
    unnamed x11, local copies, waits for them, and re-layouts  3.87 us

profile of v3, /device:TPU:17, one launch (start us, length us, event | category | flops | bytes accessed | tf_op | source)
XLA Modules:
  0.0 151.4 jit_solution(2069964637298106371)
XLA Ops:
  0.0 0.8 copy.11
  0.8 0.1 reshape_squeeze.3.refs_9_
  0.9 0.0 copy-start.3
  0.9 0.2 convert_reduce_fusion
  1.0 0.0 copy-start.2
  1.1 0.1 select_reduce_fusion.refs_7_
  2.5 0.0 copy-start.4
  2.5 0.0 copy-done.3
  2.5 0.0 copy-done.2
  2.5 0.7 copy-done.4
  3.2 0.0 copy-start
  3.2 1.2 copy-done
  4.4 0.0 copy-start.1
  4.4 1.2 copy-done.1
  5.6 144.7 %commutator.1 = f32[512,512]{1,0:T(8,128)S(1)} custom-call(f32[512,512]{1,0:T(8,128)S(1)} %bitcast.8, f32[512,512]{1,0:T(8,128)S(1)} %bitcast.9, s32[2,1024]{1,0:T(2,128)S(1)} %bitcast.10, s32[2,1024]{1,0:T(2,128)S(1)} %bitcast.11, s32[160]{0:T(256)S(1)} %copy-done.4, s32[1]{0:T(128)} %copy.12.refs_5_, s32[1]{0:T(128)S(6)} %copy.13.refs_6_, ...), custom_call_target="tpu_custom_call" | custom-call | tf_op jit(solution)/shard_map/commutator/pallas_call | solution.py:508
  150.3 1.1 select_bitcast_fusion
  (3 shorter events, 0.0 us)
Async XLA Ops:
  0.9 1.6 %copy-start.3 = (s32[1,2,1024]{2,1,0:T(2,128)S(1)}, s32[1,2,1024]{2,1,0:T(2,128)}, u32[]{:S(2)}) copy-start(s32[1,2,1024]{2,1,0:T(2,128)} %param.12) | copy-start | bytes 24580
  1.0 1.4 copy-start.2
  2.5 0.7 copy-start.4
  3.2 1.2 copy-start
  4.4 1.2 copy-start.1

commit v4 on v3

--- a/solution.py
+++ b/solution.py
@@ -392,12 +392,13 @@
 
     others(peers, send_back)
 
+    others(peers, lambda p: back_copy(p, me).start())
+
     def keep_back(k, carry):
         back_recv[me * cap + k] = product[smeta[me, 0, tiles + k]]
         return carry
 
     lax.fori_loop(0, cap, keep_back, 0, unroll=min(cap, 8))
-    others(peers, lambda p: back_copy(p, me).start())
 
     for m, ref in enumerate((gen_ref, int_ref)):
         place(

time: 152 us -> 152 us (level)
  no operation moved by 1% of the time
where the time goes in v4:
time: 152 us; the launch traced here: 151 us
  Pallas kernels  145 us (95%)
  local copies, waits for them, and re-layouts  3.96 us (3%)
    pallas_call x1, Pallas kernels, shards(): pl.pallas_call(functools.partial(kernel, static), out_shape=jax.ShapeDtyp...  145 us
    unnamed x11, local copies, waits for them, and re-layouts  3.87 us

profile of v4, /device:TPU:17, one launch (start us, length us, event | category | flops | bytes accessed | tf_op | source)
XLA Modules:
  0.0 151.3 jit_solution(6298446158181452892)
XLA Ops:
  0.0 0.8 copy.11
  0.8 0.1 reshape_squeeze.3.refs_9_
  0.9 0.0 copy-start.3
  0.9 0.2 convert_reduce_fusion
  1.0 0.0 copy-start.2
  1.1 0.1 select_reduce_fusion.refs_7_
  2.5 0.0 copy-start.4
  2.5 0.0 copy-done.3
  2.5 0.0 copy-done.2
  2.5 0.7 copy-done.4
  3.2 0.0 copy-start
  3.2 1.2 copy-done
  4.4 0.0 copy-start.1
  4.4 1.2 copy-done.1
  5.6 144.5 %commutator.1 = f32[512,512]{1,0:T(8,128)S(1)} custom-call(f32[512,512]{1,0:T(8,128)S(1)} %bitcast.8, f32[512,512]{1,0:T(8,128)S(1)} %bitcast.9, s32[2,1024]{1,0:T(2,128)S(1)} %bitcast.10, s32[2,1024]{1,0:T(2,128)S(1)} %bitcast.11, s32[160]{0:T(256)S(1)} %copy-done.4, s32[1]{0:T(128)} %copy.12.refs_5_, s32[1]{0:T(128)S(6)} %copy.13.refs_6_, ...), custom_call_target="tpu_custom_call" | custom-call | tf_op jit(solution)/shard_map/commutator/pallas_call | solution.py:509
  150.2 1.1 select_bitcast_fusion
  (3 shorter events, 0.0 us)
Async XLA Ops:
  0.9 1.6 %copy-start.3 = (s32[1,2,1024]{2,1,0:T(2,128)S(1)}, s32[1,2,1024]{2,1,0:T(2,128)}, u32[]{:S(2)}) copy-start(s32[1,2,1024]{2,1,0:T(2,128)} %param.12) | copy-start | bytes 24580
  1.0 1.4 copy-start.2
  2.5 0.7 copy-start.4
  3.2 1.2 copy-start
  4.4 1.2 copy-start.1
